TPU v7x, 32 devices: a whole 2x2x4 slice. The times are simulated.
32 devices in a mesh: sample: 8 (over z, y), space: 4 (over x, core).
Axes of the slice: x: 2, y: 2, z: 4, core: 2. Of those that a mesh axis runs over, the one named last changes fastest.
Arguments:
- features: bfloat16 [8, 64, 256, 256], P('sample', 'space'), may hold values from -6 to 6
- weight_one: bfloat16 [3, 3, 256, 256], P(None, None, None, 'sample'), may hold values from -0.125 to 0.125
- offset_one: float32 [256], replicated, may hold values from -0.5 to 0.5
- weight_two: bfloat16 [3, 3, 256, 256], P(None, None, None, 'sample'), may hold values from -0.125 to 0.125
- offset_two: float32 [256], replicated, may hold values from -0.5 to 0.5
Outputs:
- context: bfloat16 [8, 64, 256, 256], P('sample', 'space')
All inputs are finite; a program needn't handle non-finite values.
Results may differ from a plain program's by a relative error of at most 0.0047.
Values may be sent and summed in bfloat16 or wider, within the bound.
A program may use at most 192 MiB of HBM per device.

v0:
```python
import jax
import jax.numpy as jnp
from jax import lax
from jax.sharding import PartitionSpec as P

DILATION_RATE = 8


def extended(block, sides, width):
    for axis, dim in sides:
        count = lax.axis_size(axis)
        forward = [(i, i + 1) for i in range(count - 1)]
        backward = [(target, source) for source, target in forward]
        low = lax.ppermute(
            lax.slice_in_dim(block, block.shape[dim] - width, None, axis=dim), axis, forward
        )
        high = lax.ppermute(lax.slice_in_dim(block, 0, width, axis=dim), axis, backward)
        block = jnp.concatenate([low, block, high], axis=dim)
    return block


def dilated(padded_input, kernel_weights, output_rows):
    tile_width = padded_input.shape[2]
    column_count = jnp.pad(padded_input, ((0, 0), (0, 0), (DILATION_RATE, DILATION_RATE), (0, 0)))
    tap_sum = None
    for row_offset_tap in range(3):
        for column_offset_tap in range(3):
            window = column_count[
                :,
                row_offset_tap * DILATION_RATE : row_offset_tap * DILATION_RATE + output_rows,
                column_offset_tap * DILATION_RATE : column_offset_tap * DILATION_RATE + tile_width,
                :,
            ]
            product = jnp.einsum(
                "shwc,co->shwo",
                window,
                kernel_weights[row_offset_tap, column_offset_tap],
                preferred_element_type=jnp.float32,
            )
            tap_sum = product if tap_sum is None else tap_sum + product
    return tap_sum


def first_layer(padded_input, weight_one, gathered, output_rows):
    gathered = lax.all_gather(weight_one, "sample", axis=3, tiled=True)
    return dilated(padded_input, gathered, output_rows)


def second_layer(padded_input, weight_two, gathered, output_rows):
    gathered = lax.all_gather(weight_two, "sample", axis=3, tiled=True)
    return dilated(padded_input, gathered, output_rows)


def with_rim(feature_values):
    return extended(feature_values, (("space", 1),), DILATION_RATE)


def per_device(features, weight_one, offset_one, weight_two, offset_two):
    rows_dev = features.shape[1]
    kernel_one, kernel_two = (None, None)
    tap_sum = first_layer(with_rim(features), weight_one, kernel_one, rows_dev)
    hidden = jnp.maximum(tap_sum + offset_one, 0.0).astype(jnp.bfloat16)
    hidden_rows = with_rim(hidden)
    result = second_layer(hidden_rows, weight_two, kernel_two, rows_dev)
    return jnp.maximum(result + offset_two, 0.0).astype(jnp.bfloat16)


def solution(mesh):
    return jax.shard_map(
        per_device,
        mesh=mesh,
        in_specs=(
            P("sample", "space", None, None),
            P(None, None, None, "sample"),
            P(),
            P(None, None, None, "sample"),
            P(),
        ),
        out_specs=P("sample", "space", None, None),
        check_vma=False,
    )
```

profile of v0, /device:TPU:1, one launch (start us, length us, event | category | flops | bytes accessed | tf_op | source)
XLA Modules:
  0.0 146.6 jit_solution(10417974059888261316)
XLA Ops:
  6.5 0.7 all-gather.3.cloned.1.call-update
  7.3 3.1 %fusion.43 = (bf16[1,8,256,256]{3,2,1,0:T(8,128)(2,1)}, bf16[1,8,256,256]{3,2,1,0:T(8,128)(2,1)}) fusion(bf16[1,16,256,256]{3,2,1,0:T(8,128)(2,1)} %param.5), kind=kLoop, calls=%fused_computation.79 | loop fusion | bytes 4194304 | tf_op jit(solution)/shard_map/slice | solution.py:15
  10.4 4.5 %collective-permute-start = (bf16[1,8,256,256]{3,2,1,0:T(8,128)(2,1)}, bf16[1,8,256,256]{3,2,1,0:T(8,128)(2,1)S(1)}, u32[]{:S(2)}, u32[]{:S(2)}) collective-permute-start(bf16[1,8,256,256]{3,2,1,0:T(8,128)(2,1)} %get-tuple-element.7), channel_id=1, source_target_pairs={{0,1},{1,2},{2,3},{4,5},{5,6},{6,7},{8,9},{9,10},{10,11},{12,13},{... | collective-permute-start | bytes 3145736 | tf_op jit(solution)/shard_map/ppermute | solution.py:14
  14.9 1.9 %collective-permute-start.1 = (bf16[1,8,256,256]{3,2,1,0:T(8,128)(2,1)}, bf16[1,8,256,256]{3,2,1,0:T(8,128)(2,1)}, u32[]{:S(2)}, u32[]{:S(2)}) collective-permute-start(bf16[1,8,256,256]{3,2,1,0:T(8,128)(2,1)} %get-tuple-element.8), channel_id=1, source_target_pairs={{1,0},{2,1},{3,2},{5,4},{6,5},{7,6},{9,8},{10,9},{11,10},{13,12},{... | collective-permute-start | bytes 3145736 | tf_op jit(solution)/shard_map/ppermute | solution.py:17
  16.8 10.1 %collective-permute-done = bf16[1,8,256,256]{3,2,1,0:T(8,128)(2,1)S(1)} collective-permute-done((bf16[1,8,256,256]{3,2,1,0:T(8,128)(2,1)}, bf16[1,8,256,256]{3,2,1,0:T(8,128)(2,1)S(1)}, u32[]{:S(2)}, u32[]{:S(2)}) %collective-permute-start) | collective-permute-done | bytes 1048608 | tf_op jit(solution)/shard_map/ppermute | solution.py:14
  26.9 4.7 %collective-permute-done.1 = bf16[1,8,256,256]{3,2,1,0:T(8,128)(2,1)} collective-permute-done((bf16[1,8,256,256]{3,2,1,0:T(8,128)(2,1)}, bf16[1,8,256,256]{3,2,1,0:T(8,128)(2,1)}, u32[]{:S(2)}, u32[]{:S(2)}) %collective-permute-start.1) | collective-permute-done | bytes 1048608 | tf_op jit(solution)/shard_map/ppermute | solution.py:17
  31.6 3.5 %fusion.5 = bf16[1,32,272,256]{3,2,1,0:T(8,128)(2,1)} fusion(bf16[1,8,256,256]{3,2,1,0:T(8,128)(2,1)} %collective-permute-done.1, bf16[1,16,256,256]{3,2,1,0:T(8,128)(2,1)S(1)} %copy-done.1, bf16[1,8,256,256]{3,2,1,0:T(8,128)(2,1)S(1)} %collective-permute-done), kind=kLoop, calls=%fused_computation.9 | loop fusion | flops 26738688 | bytes 8650752 | tf_op jit(solution)/shard_map/concatenate | solution.py:18
  35.1 16.4 %all-gather.3.cloned.1.call-done = bf16[3,3,256,256]{2,3,1,0:T(8,128)(2,1)} async-done(((bf16[3,3,256,32]{2,3,1,0:T(8,128)(2,1)}), bf16[3,3,256,256]{2,3,1,0:T(8,128)(2,1)}) %all-gather.3.cloned.1.call-update) | async-done | bytes 1179664 | tf_op jit(solution)/shard_map/all_gather | solution.py:45
  51.5 4.5 %fusion.25 = f32[16,256,256]{2,1,0:T(8,128)} fusion(bf16[1,32,272,256]{3,2,1,0:T(8,128)(2,1)} %fusion.5, bf16[3,3,256,256]{2,3,1,0:T(8,128)(2,1)} %all-gather.3.cloned.1.call-done), kind=kOutput, calls=%fused_computation.39 | convolution fusion | flops 536870912 | bytes 6422528 | tf_op jit(solution)/shard_map/shwc,co->shwo/dot_general | solution.py:34
  56.1 2.7 %fusion.26 = f32[16,256,256]{2,1,0:T(8,128)} fusion(bf16[1,32,272,256]{3,2,1,0:T(8,128)(2,1)S(1)} %copy-done, bf16[3,3,256,256]{2,3,1,0:T(8,128)(2,1)S(1)} %copy-done.6), kind=kOutput, calls=%fused_computation.41 | convolution fusion | flops 536870912 | bytes 6422528 | tf_op jit(solution)/shard_map/shwc,co->shwo/dot_general | solution.py:34
  58.8 2.7 %fusion.27 = f32[16,256,256]{2,1,0:T(8,128)} fusion(bf16[1,32,272,256]{3,2,1,0:T(8,128)(2,1)S(1)} %copy-done, bf16[3,3,256,256]{2,3,1,0:T(8,128)(2,1)S(1)} %copy-done.6), kind=kOutput, calls=%fused_computation.43 | convolution fusion | flops 536870912 | bytes 6422528 | tf_op jit(solution)/shard_map/shwc,co->shwo/dot_general | solution.py:34
  61.5 2.7 %fusion.28 = f32[16,256,256]{2,1,0:T(8,128)} fusion(bf16[1,32,272,256]{3,2,1,0:T(8,128)(2,1)S(1)} %copy-done, bf16[3,3,256,256]{2,3,1,0:T(8,128)(2,1)S(1)} %copy-done.6), kind=kOutput, calls=%fused_computation.45 | convolution fusion | flops 536870912 | bytes 6422528 | tf_op jit(solution)/shard_map/shwc,co->shwo/dot_general | solution.py:34
  64.2 2.7 %fusion.33 = f32[16,256,256]{2,1,0:T(8,128)} fusion(bf16[1,32,272,256]{3,2,1,0:T(8,128)(2,1)S(1)} %copy-done, bf16[3,3,256,256]{2,3,1,0:T(8,128)(2,1)S(1)} %copy-done.6), kind=kOutput, calls=%fused_computation.51 | convolution fusion | flops 536870912 | bytes 6422528 | tf_op jit(solution)/shard_map/shwc,co->shwo/dot_general | solution.py:34
  66.9 2.1 %fusion.22 = f32[16,256,256]{2,1,0:T(8,128)S(1)} fusion(bf16[1,8,256,256]{3,2,1,0:T(8,128)(2,1)} %collective-permute-done.1, bf16[1,16,256,256]{3,2,1,0:T(8,128)(2,1)S(1)} %copy-done.1, bf16[3,3,256,256]{2,3,1,0:T(8,128)(2,1)S(1)} %copy-done.6), kind=kOutput, calls=%fused_computation.36 | convolution fusion | flops 537919488 | bytes 7471104 | tf_op jit(solution)/shard_map/shwc,co->shwo/dot_general | solution.py:34
  68.9 2.7 %fusion.30 = f32[16,256,256]{2,1,0:T(8,128)} fusion(bf16[1,16,256,256]{3,2,1,0:T(8,128)(2,1)S(1)} %copy-done.1, bf16[1,8,256,256]{3,2,1,0:T(8,128)(2,1)S(1)} %copy-done.3, bf16[3,3,256,256]{2,3,1,0:T(8,128)(2,1)S(1)} %copy-done.6), kind=kOutput, calls=%fused_computation.48 | convolution fusion | flops 537919488 | bytes 7471104 | tf_op jit(solution)/shard_map/shwc,co->shwo/dot_general | solution.py:34
  71.7 2.8 %fusion.34 = f32[16,256,256]{2,1,0:T(8,128)} fusion(bf16[1,16,256,256]{3,2,1,0:T(8,128)(2,1)S(1)} %copy-done.1, bf16[3,3,256,256]{2,3,1,0:T(8,128)(2,1)S(1)} %copy-done.6), kind=kOutput, calls=%fused_computation.52 | convolution fusion | flops 536870912 | bytes 6422528 | tf_op jit(solution)/shard_map/shwc,co->shwo/dot_general | solution.py:34
  74.5 10.8 %maximum_convert_fusion.1 = bf16[16,256,256]{2,1,0:T(8,128)(2,1)S(1)} fusion(f32[16,256,256]{2,1,0:T(8,128)S(1)} %fusion.22, f32[16,256,256]{2,1,0:T(8,128)} %fusion.25, f32[16,256,256]{2,1,0:T(8,128)} %fusion.26, f32[16,256,256]{2,1,0:T(8,128)} %fusion.34, f32[16,256,256]{2,1,0:T(8,128)} %fusion.27, f32[16,256,256]{2,1,0:T(8,128)} %fusion.28, ...), kind=kOutput, calls=%fused_computation.11 | convolution fusion | flops 548405248 | bytes 37880832 | tf_op jit(solution)/shard_map/shwc,co->shwo/dot_general | solution.py:34
  85.3 1.5 %fusion.42 = (bf16[1,8,256,256]{3,2,1,0:T(8,128)(2,1)}, bf16[1,8,256,256]{3,2,1,0:T(8,128)(2,1)}) fusion(bf16[1,16,256,256]{3,2,1,0:T(8,128)(2,1)S(1)} %bitcast.169), kind=kLoop, calls=%fused_computation.78 | loop fusion | bytes 4194304 | tf_op jit(solution)/shard_map/slice | solution.py:15
  86.8 4.9 %collective-permute-start.2 = (bf16[1,8,256,256]{3,2,1,0:T(8,128)(2,1)}, bf16[1,8,256,256]{3,2,1,0:T(8,128)(2,1)S(1)}, u32[]{:S(2)}, u32[]{:S(2)}) collective-permute-start(bf16[1,8,256,256]{3,2,1,0:T(8,128)(2,1)} %get-tuple-element.5), channel_id=1, source_target_pairs={{0,1},{1,2},{2,3},{4,5},{5,6},{6,7},{8,9},{9,10},{10,11},{12,13},{... | collective-permute-start | bytes 3145736 | tf_op jit(solution)/shard_map/ppermute | solution.py:14
  91.7 2.1 %collective-permute-start.3 = (bf16[1,8,256,256]{3,2,1,0:T(8,128)(2,1)}, bf16[1,8,256,256]{3,2,1,0:T(8,128)(2,1)}, u32[]{:S(2)}, u32[]{:S(2)}) collective-permute-start(bf16[1,8,256,256]{3,2,1,0:T(8,128)(2,1)} %get-tuple-element.6), channel_id=1, source_target_pairs={{1,0},{2,1},{3,2},{5,4},{6,5},{7,6},{9,8},{10,9},{11,10},{13,12},{... | collective-permute-start | bytes 3145736 | tf_op jit(solution)/shard_map/ppermute | solution.py:17
  93.8 3.7 %fusion.37 = f32[16,256,256]{2,1,0:T(8,128)} fusion(bf16[16,256,256]{2,1,0:T(8,128)(2,1)S(1)} %maximum_convert_fusion.1, bf16[3,3,256,256]{2,3,1,0:T(8,128)(2,1)} %all-gather.5.cloned.1.call-done), kind=kOutput, calls=%fused_computation.60 | convolution fusion | flops 536870912 | bytes 6422528 | tf_op jit(solution)/shard_map/shwc,co->shwo/dot_general | solution.py:34
  97.5 6.2 %collective-permute-done.2 = bf16[1,8,256,256]{3,2,1,0:T(8,128)(2,1)S(1)} collective-permute-done((bf16[1,8,256,256]{3,2,1,0:T(8,128)(2,1)}, bf16[1,8,256,256]{3,2,1,0:T(8,128)(2,1)S(1)}, u32[]{:S(2)}, u32[]{:S(2)}) %collective-permute-start.2) | collective-permute-done | bytes 1048608 | tf_op jit(solution)/shard_map/ppermute | solution.py:14
  103.7 0.7 fusion.16
  104.7 3.4 %collective-permute-done.3 = bf16[1,8,256,256]{3,2,1,0:T(8,128)(2,1)} collective-permute-done((bf16[1,8,256,256]{3,2,1,0:T(8,128)(2,1)}, bf16[1,8,256,256]{3,2,1,0:T(8,128)(2,1)}, u32[]{:S(2)}, u32[]{:S(2)}) %collective-permute-start.3) | collective-permute-done | bytes 1048608 | tf_op jit(solution)/shard_map/ppermute | solution.py:17
  108.1 2.1 %select_maximum_fusion = bf16[1,32,272,256]{3,2,1,0:T(8,128)(2,1)S(1)} fusion(bf16[1,8,256,256]{3,2,1,0:T(8,128)(2,1)} %collective-permute-done.3, bf16[1,16,256,256]{3,2,1,0:T(8,128)(2,1)S(1)} %bitcast.171, bf16[1,8,256,256]{3,2,1,0:T(8,128)(2,1)} %copy-done.4), kind=kLoop, calls=%fused_computation.3 | loop fusion | flops 26738688 | bytes 8650752 | tf_op jit(solution)/shard_map/concatenate | solution.py:18
  110.2 2.7 %fusion.11 = f32[16,256,256]{2,1,0:T(8,128)} fusion(bf16[1,32,272,256]{3,2,1,0:T(8,128)(2,1)S(1)} %select_maximum_fusion, bf16[3,3,256,256]{2,3,1,0:T(8,128)(2,1)S(1)} %copy-done.5), kind=kOutput, calls=%fused_computation.19 | convolution fusion | flops 536870912 | bytes 6422528 | tf_op jit(solution)/shard_map/shwc,co->shwo/dot_general | solution.py:34
  112.9 2.7 %fusion.12 = f32[16,256,256]{2,1,0:T(8,128)} fusion(bf16[1,32,272,256]{3,2,1,0:T(8,128)(2,1)S(1)} %select_maximum_fusion, bf16[3,3,256,256]{2,3,1,0:T(8,128)(2,1)S(1)} %copy-done.5), kind=kOutput, calls=%fused_computation.21 | convolution fusion | flops 536870912 | bytes 6422528 | tf_op jit(solution)/shard_map/shwc,co->shwo/dot_general | solution.py:34
  115.6 2.7 %fusion.13 = f32[16,256,256]{2,1,0:T(8,128)} fusion(bf16[1,32,272,256]{3,2,1,0:T(8,128)(2,1)S(1)} %select_maximum_fusion, bf16[3,3,256,256]{2,3,1,0:T(8,128)(2,1)S(1)} %copy-done.5), kind=kOutput, calls=%fused_computation.23 | convolution fusion | flops 536870912 | bytes 6422528 | tf_op jit(solution)/shard_map/shwc,co->shwo/dot_general | solution.py:34
  118.3 2.7 %fusion.14 = f32[16,256,256]{2,1,0:T(8,128)} fusion(bf16[1,32,272,256]{3,2,1,0:T(8,128)(2,1)S(1)} %select_maximum_fusion, bf16[3,3,256,256]{2,3,1,0:T(8,128)(2,1)S(1)} %copy-done.5), kind=kOutput, calls=%fused_computation.25 | convolution fusion | flops 536870912 | bytes 6422528 | tf_op jit(solution)/shard_map/shwc,co->shwo/dot_general | solution.py:34
  121.0 2.7 %fusion.19 = f32[16,256,256]{2,1,0:T(8,128)} fusion(bf16[1,32,272,256]{3,2,1,0:T(8,128)(2,1)S(1)} %select_maximum_fusion, bf16[3,3,256,256]{2,3,1,0:T(8,128)(2,1)S(1)} %copy-done.5), kind=kOutput, calls=%fused_computation.31 | convolution fusion | flops 536870912 | bytes 6422528 | tf_op jit(solution)/shard_map/shwc,co->shwo/dot_general | solution.py:34
  123.7 4.0 %fusion.8 = f32[16,256,256]{2,1,0:T(8,128)} fusion(bf16[1,8,256,256]{3,2,1,0:T(8,128)(2,1)} %collective-permute-done.3, bf16[1,16,256,256]{3,2,1,0:T(8,128)(2,1)S(1)} %bitcast.172, bf16[3,3,256,256]{2,3,1,0:T(8,128)(2,1)S(1)} %copy-done.5), kind=kOutput, calls=%fused_computation.16 | convolution fusion | flops 537919488 | bytes 7471104 | tf_op jit(solution)/shard_map/shwc,co->shwo/dot_general | solution.py:34
  127.7 12.1 %fusion.36 = bf16[1,16,256,256]{3,2,1,0:T(8,128)(2,1)} fusion(f32[256]{0:T(256)S(1)} %copy-done.8, bf16[1,32,272,256]{3,2,1,0:T(8,128)(2,1)S(1)} %select_maximum_fusion, f32[16,256,256]{2,1,0:T(8,128)} %fusion.8, f32[16,256,256]{2,1,0:T(8,128)} %fusion.11, f32[16,256,256]{2,1,0:T(8,128)} %fusion.12, f32[16,256,256]{2,1,0:T(8,128)} %fusion.37, ...), kind=kOutput, calls=%fused_computation.54 | convolution fusion | flops 548405248 | bytes 37880832 | tf_op jit(solution)/shard_map/shwc,co->shwo/dot_general | solution.py:34
  (22 shorter events, 0.3 us)
Async XLA Ops:
  6.5 25.1 %copy-start.1 = (bf16[1,16,256,256]{3,2,1,0:T(8,128)(2,1)S(1)}, bf16[1,16,256,256]{3,2,1,0:T(8,128)(2,1)}, u32[]{:S(2)}) copy-start(bf16[1,16,256,256]{3,2,1,0:T(8,128)(2,1)} %param.5) | copy-start | bytes 6291460
  6.5 45.0 %all-gather.3.cloned.1.call-start = ((), (), s32[]{:S(2)}) async-start(), calls=%async_computation | async-start | bytes 1327104 | tf_op jit(solution)/shard_map/all_gather | solution.py:45
  7.3 86.6 %all-gather.5.cloned.1.call-start = ((), (), s32[]{:S(2)}) async-start(), calls=%async_computation.1 | async-start | bytes 1327104 | tf_op jit(solution)/shard_map/all_gather | solution.py:50
  10.4 16.5 %collective-permute-start = (bf16[1,8,256,256]{3,2,1,0:T(8,128)(2,1)}, bf16[1,8,256,256]{3,2,1,0:T(8,128)(2,1)S(1)}, u32[]{:S(2)}, u32[]{:S(2)}) collective-permute-start(bf16[1,8,256,256]{3,2,1,0:T(8,128)(2,1)} %get-tuple-element.7), channel_id=1, source_target_pairs={{0,1},{1,2},{2,3},{4,5},{5,6},{6,7},{8,9},{9,10},{10,11},{12,13},{... | collective-permute-start | bytes 3145736 | tf_op jit(solution)/shard_map/ppermute | solution.py:14
  14.9 16.7 %collective-permute-start.1 = (bf16[1,8,256,256]{3,2,1,0:T(8,128)(2,1)}, bf16[1,8,256,256]{3,2,1,0:T(8,128)(2,1)}, u32[]{:S(2)}, u32[]{:S(2)}) collective-permute-start(bf16[1,8,256,256]{3,2,1,0:T(8,128)(2,1)} %get-tuple-element.8), channel_id=1, source_target_pairs={{1,0},{2,1},{3,2},{5,4},{6,5},{7,6},{9,8},{10,9},{11,10},{13,12},{... | collective-permute-start | bytes 3145736 | tf_op jit(solution)/shard_map/ppermute | solution.py:17
  26.9 8.2 %copy-start.2 = (bf16[1,8,256,256]{3,2,1,0:T(8,128)(2,1)}, bf16[1,8,256,256]{3,2,1,0:T(8,128)(2,1)S(1)}, u32[]{:S(2)}) copy-start(bf16[1,8,256,256]{3,2,1,0:T(8,128)(2,1)S(1)} %collective-permute-done) | copy-start | bytes 3145732
  51.5 4.5 %copy-start = (bf16[1,32,272,256]{3,2,1,0:T(8,128)(2,1)S(1)}, bf16[1,32,272,256]{3,2,1,0:T(8,128)(2,1)}, u32[]{:S(2)}) copy-start(bf16[1,32,272,256]{3,2,1,0:T(8,128)(2,1)} %fusion.5) | copy-start | bytes 13369348
  51.5 4.5 %copy-start.6 = (bf16[3,3,256,256]{2,3,1,0:T(8,128)(2,1)S(1)}, bf16[3,3,256,256]{2,3,1,0:T(8,128)(2,1)}, u32[]{:S(2)}) copy-start(bf16[3,3,256,256]{2,3,1,0:T(8,128)(2,1)} %all-gather.3.cloned.1.call-done) | copy-start | bytes 3538948
  66.9 2.1 %copy-start.3 = (bf16[1,8,256,256]{3,2,1,0:T(8,128)(2,1)S(1)}, bf16[1,8,256,256]{3,2,1,0:T(8,128)(2,1)}, u32[]{:S(2)}) copy-start(bf16[1,8,256,256]{3,2,1,0:T(8,128)(2,1)} %copy-done.2) | copy-start | bytes 3145732
  71.7 2.8 %copy-start.7 = (f32[256]{0:T(256)S(1)}, f32[256]{0:T(256)}, u32[]{:S(2)}) copy-start(f32[256]{0:T(256)} %param.7) | copy-start | bytes 3076
  86.8 16.9 %collective-permute-start.2 = (bf16[1,8,256,256]{3,2,1,0:T(8,128)(2,1)}, bf16[1,8,256,256]{3,2,1,0:T(8,128)(2,1)S(1)}, u32[]{:S(2)}, u32[]{:S(2)}) collective-permute-start(bf16[1,8,256,256]{3,2,1,0:T(8,128)(2,1)} %get-tuple-element.5), channel_id=1, source_target_pairs={{0,1},{1,2},{2,3},{4,5},{5,6},{6,7},{8,9},{9,10},{10,11},{12,13},{... | collective-permute-start | bytes 3145736 | tf_op jit(solution)/shard_map/ppermute | solution.py:14
  91.7 16.4 %collective-permute-start.3 = (bf16[1,8,256,256]{3,2,1,0:T(8,128)(2,1)}, bf16[1,8,256,256]{3,2,1,0:T(8,128)(2,1)}, u32[]{:S(2)}, u32[]{:S(2)}) collective-permute-start(bf16[1,8,256,256]{3,2,1,0:T(8,128)(2,1)} %get-tuple-element.6), channel_id=1, source_target_pairs={{1,0},{2,1},{3,2},{5,4},{6,5},{7,6},{9,8},{10,9},{11,10},{13,12},{... | collective-permute-start | bytes 3145736 | tf_op jit(solution)/shard_map/ppermute | solution.py:17
  93.8 9.9 %copy-start.5 = (bf16[3,3,256,256]{2,3,1,0:T(8,128)(2,1)S(1)}, bf16[3,3,256,256]{2,3,1,0:T(8,128)(2,1)}, u32[]{:S(2)}) copy-start(bf16[3,3,256,256]{2,3,1,0:T(8,128)(2,1)} %all-gather.5.cloned.1.call-done) | copy-start | bytes 3538948
  103.7 1.0 copy-start.4
  123.7 4.0 %copy-start.8 = (f32[256]{0:T(256)S(1)}, f32[256]{0:T(256)}, u32[]{:S(2)}) copy-start(f32[256]{0:T(256)} %param.9) | copy-start | bytes 3076
Sparse Core Ops, SparseCore 0:
  9.5 41.9 all-gather.2
  53.7 39.8 all-gather.4
where the time goes:
time: 147 us
  matrix products  67.7 us (46%)
  waiting for transfers between devices  41.6 us (28%)
  starting transfers between devices  13.5 us (9%)
  between operations  13.5 us (9%)
  other arithmetic  5.53 us (4%)
  local copies, waits for them, and re-layouts  4.85 us (3%)
    dot_general x18, matrix products, dilated(): jnp.einsum('shwc,co->shwo', window, kernel_weights[row_offset_tap, column...  67.7 us
    all_gather x1, waiting for transfers between devices, first_layer(): gathered = lax.all_gather(weight_one, 'sample', axis=3, tiled=True)  16.4 us
    ppermute x2, waiting for transfers between devices, extended(): lax.ppermute(lax.slice_in_dim(block, block.shape[dim] - width, None, axis...  16.3 us
    ppermute x2, starting transfers between devices, extended(): lax.ppermute(lax.slice_in_dim(block, block.shape[dim] - width, None, axis...  9.39 us
    ppermute x2, waiting for transfers between devices, extended(): lax.ppermute(lax.slice_in_dim(block, 0, width, axis=dim), axis, backward)  8.11 us
    concatenate x2, other arithmetic, extended(): block = jnp.concatenate([low, block, high], axis=dim)  5.53 us
    slice x2, local copies, waits for them, and re-layouts, extended(): lax.slice_in_dim(block, block.shape[dim] - width, None, axis=dim)  4.59 us
    ppermute x2, starting transfers between devices, extended(): lax.ppermute(lax.slice_in_dim(block, 0, width, axis=dim), axis, backward)  4.02 us
  transfers between devices with their start and end apart: 6, of which 5 were waited for; matrix products, arithmetic and copies ran while one was open for 31% of the time, Pallas kernels for 0%

commit v1 on v0

v1 whole, which is shorter than its diff:
```python
import functools

import jax
import jax.numpy as jnp
from jax import lax
from jax.experimental import pallas as pl
from jax.experimental.pallas import tpu as pltpu
from jax.sharding import PartitionSpec as P

MESH = pl.DeviceIdType.MESH
D = 8
R = 2


def kernel(
    n_sample, n_space, f_ref, w1_ref, w2_ref, b1_ref, b2_ref, out_ref,
    x, h, wloc, wt, obuf,
    loc_sem, out_sem, bar_unused,
    near_sem, far_s, far_r, hnear_s, hnear_r, hfar_s, hfar_r,
    z_s, z_r, y_s, y_r, c_s, c_r,
):
    rows, width, chans = out_ref.shape[1:]
    chunks = D // R
    n_hi = n_sample // 2
    o_loc = wloc.shape[-1]
    half = chans // 2
    space = lax.axis_index("space")
    sample = lax.axis_index("sample")
    odd = lax.rem(space, 2)
    hi, lo = sample // 2, lax.rem(sample, 2)

    near = space + 1 - 2 * odd
    far = space - 1 + 2 * odd
    has_far = jnp.logical_and(far >= 0, far < n_space)
    far_group, near_group = 1 + odd, 2 - odd
    far_halo, near_halo = 3 * D * odd, 3 * D * (1 - odd)

    feat_in = pltpu.make_async_copy(f_ref.at[0], x.at[pl.ds(D, rows)], loc_sem.at[0])
    w_in = [
        pltpu.make_async_copy(w, wloc.at[l], loc_sem.at[1 + l])
        for l, w in enumerate((w1_ref, w2_ref))
    ]
    w_in[0].start()
    w_in[1].start()
    feat_in.start()

    barrier = pltpu.get_barrier_semaphore()
    peers = [{"space": near}, {"sample": hi * 2 + 1 - lo}]
    peers += [{"sample": lax.rem(hi + k, n_hi) * 2 + lo} for k in range(1, n_hi)]
    for peer in peers:
        pl.semaphore_signal(barrier, inc=1, device_id=peer, device_id_type=MESH)

    @pl.when(has_far)
    def _():
        pl.semaphore_signal(barrier, inc=1, device_id={"space": far}, device_id_type=MESH)
        pl.semaphore_wait(barrier, len(peers) + 1)

    @pl.when(jnp.logical_not(has_far))
    def _():
        pl.semaphore_wait(barrier, len(peers))

    def remote(src, dst, send, recv, peer):
        return pltpu.make_async_remote_copy(
            src_ref=src, dst_ref=dst, send_sem=send, recv_sem=recv,
            device_id=peer, device_id_type=MESH,
        )

    def feat_far(i):
        return remote(
            f_ref.at[0, pl.ds(D * odd + R * i, R)],
            x.at[pl.ds(3 * D * (1 - odd) + R * i, R)],
            far_s.at[i], far_r.at[i], {"space": far},
        )

    def hid_far(i):
        return remote(
            h.at[pl.ds(D * far_group + R * i, R)],
            h.at[pl.ds(3 * D * (1 - odd) + R * i, R)],
            hfar_s.at[i], hfar_r.at[i], {"space": far},
        )

    feat_near = remote(
        f_ref.at[0, pl.ds(D * (1 - odd), D)],
        x.at[pl.ds(3 * D * odd, D)],
        near_sem.at[0], near_sem.at[1], {"space": near},
    )

    def hid_near(i):
        return remote(
            h.at[pl.ds(D * near_group + R * i, R)],
            h.at[pl.ds(3 * D * odd + R * i, R)],
            hnear_s.at[i], hnear_r.at[i], {"space": near},
        )

    @pl.when(has_far)
    def _():
        for i in range(chunks):
            feat_far(i).start()

    def piece(l, k, q, which):
        owner = lax.rem(hi - k + n_hi, n_hi) * 2 + (lo if q == 0 else 1 - lo)
        start = pl.multiple_of(owner * o_loc, o_loc)
        lane = pl.multiple_of(which * half, half)
        return wt.at[l, :, pl.ds(start, o_loc), pl.ds(lane, half)]

    def z_copy(l, k):
        ref = piece(l, 0, 0, odd)
        return remote(ref, ref, z_s.at[l, k], z_r.at[l, k], {"sample": lax.rem(hi + k, n_hi) * 2 + lo})

    def z_arrived(l, k):
        ref = piece(l, k, 0, odd)
        return remote(ref, ref, z_s.at[l, k], z_r.at[l, k], {"sample": lax.rem(hi + k, n_hi) * 2 + lo})

    def y_copy(l, k):
        ref = piece(l, k, 0, odd)
        return remote(ref, ref, y_s.at[l, k], y_r.at[l, k], {"sample": hi * 2 + 1 - lo})

    def y_arrived(l, k):
        ref = piece(l, k, 1, odd)
        return remote(ref, ref, y_s.at[l, k], y_r.at[l, k], {"sample": hi * 2 + 1 - lo})

    def c_copy(l, k, q):
        ref = piece(l, k, q, odd)
        return remote(ref, ref, c_s.at[l, k, q], c_r.at[l, k, q], {"space": near})

    def c_arrived(l, k, q):
        ref = piece(l, k, q, 1 - odd)
        return remote(ref, ref, c_s.at[l, k, q], c_r.at[l, k, q], {"space": near})

    def scatter(l):
        w_in[l].wait()
        start = pl.multiple_of(sample * o_loc, o_loc)
        for a in range(3):
            for b in range(3):
                wt[l, 3 * a + b, pl.ds(start, o_loc), :] = wloc[l, a, b].T
        for k in range(1, n_hi):
            z_copy(l, k).start()
        y_copy(l, 0).start()

    def forward_z(l):
        for k in range(1, n_hi):
            z_arrived(l, k).wait_recv()
            y_copy(l, k).start()
            c_copy(l, k, 0).start()

    def forward_y(l):
        for k in range(n_hi):
            y_arrived(l, k).wait_recv()
            c_copy(l, k, 1).start()

    def collect(l):
        for k in range(n_hi):
            for q in range(2):
                if (k, q) != (0, 0):
                    c_arrived(l, k, q).wait_recv()

    def sent(l):
        for k in range(n_hi):
            y_copy(l, k).wait_send()
            if k:
                z_copy(l, k).wait_send()
            for q in range(2):
                if (k, q) != (0, 0):
                    c_copy(l, k, q).wait_send()

    scatter(0)
    feat_near.start()
    scatter(1)

    @pl.when(jnp.logical_not(has_far))
    def _():
        zero = jnp.zeros((D, width, chans), jnp.bfloat16)
        x[pl.ds(far_halo, D)] = zero
        h[pl.ds(far_halo, D)] = zero

    forward_z(0)
    forward_y(0)
    feat_in.wait()
    feat_near.wait_recv()
    collect(0)

    def conv_rows(src, l, bias, group, i):
        lhs = jnp.concatenate(
            [src[pl.ds(D * (group + a - 1) + R * i, R)].reshape(R * width, chans) for a in range(3)], axis=1
        )
        ys = []
        for b in range(3):
            rhs = jnp.concatenate([wt[l, 3 * a + b] for a in range(3)], axis=1)
            y = lax.dot_general(lhs, rhs, (((1,), (1,)), ((), ())), preferred_element_type=jnp.float32)
            ys.append(y.reshape(R, width, chans))
        zero = jnp.zeros((R, D, chans), jnp.float32)
        low = jnp.concatenate([zero, ys[0][:, : width - D]], axis=1)
        high = jnp.concatenate([ys[2][:, D:], zero], axis=1)
        total = ys[1] + low + high + bias[...].reshape(1, 1, chans)
        return jnp.maximum(total, 0.0).astype(jnp.bfloat16)

    def hidden_far(i, carry):
        @pl.when(has_far)
        def _():
            feat_far(i).wait_recv()

        h[pl.ds(D * far_group + R * i, R)] = conv_rows(x, 0, b1_ref, far_group, i)

        @pl.when(has_far)
        def _():
            hid_far(i).start()

        return carry

    def hidden_near(i, carry):
        h[pl.ds(D * near_group + R * i, R)] = conv_rows(x, 0, b1_ref, near_group, i)
        hid_near(i).start()
        return carry

    def put(group, i):
        row = D * (group - 1) + R * i
        return pltpu.make_async_copy(
            obuf.at[pl.ds(row, R)], out_ref.at[0, pl.ds(row, R)], out_sem.at[group - 1, i]
        )

    def context_near(i, carry):
        hid_near(i).wait_recv()
        obuf[pl.ds(D * (near_group - 1) + R * i, R)] = conv_rows(h, 1, b2_ref, near_group, i)
        put(near_group, i).start()
        return carry

    def context_far(i, carry):
        @pl.when(has_far)
        def _():
            hid_far(i).wait_recv()

        obuf[pl.ds(D * (far_group - 1) + R * i, R)] = conv_rows(h, 1, b2_ref, far_group, i)
        put(far_group, i).start()
        return carry

    lax.fori_loop(0, chunks, hidden_far, 0)
    forward_z(1)
    lax.fori_loop(0, chunks, hidden_near, 0)
    forward_y(1)
    collect(1)
    lax.fori_loop(0, chunks, context_near, 0)
    lax.fori_loop(0, chunks, context_far, 0)

    feat_near.wait_send()
    sent(0)
    sent(1)
    for i in range(chunks):
        hid_near(i).wait_send()

    @pl.when(has_far)
    def _():
        for i in range(chunks):
            feat_far(i).wait_send()
            hid_far(i).wait_send()

    for i in range(chunks):
        put(near_group, i).wait()
        put(far_group, i).wait()


def solution(mesh):
    n_sample, n_space = mesh.shape["sample"], mesh.shape["space"]
    assert n_sample % 2 == 0 and n_space % 2 == 0

    def per_device(features, weight_one, offset_one, weight_two, offset_two):
        _, rows, width, chans = features.shape
        assert features.shape[0] == 1 and rows == 2 * D
        o_loc = weight_one.shape[-1]
        n_hi, chunks = n_sample // 2, D // R
        bf16, dma = jnp.bfloat16, pltpu.SemaphoreType.DMA
        anywhere = pl.BlockSpec(memory_space=pl.ANY)
        vmem = pl.BlockSpec(memory_space=pltpu.VMEM)
        return pl.pallas_call(
            functools.partial(kernel, n_sample, n_space),
            out_shape=jax.ShapeDtypeStruct(features.shape, bf16),
            in_specs=[anywhere, anywhere, anywhere, vmem, vmem],
            out_specs=anywhere,
            scratch_shapes=[
                pltpu.VMEM((4 * D, width, chans), bf16),
                pltpu.VMEM((4 * D, width, chans), bf16),
                pltpu.VMEM((2, 3, 3, chans, o_loc), bf16),
                pltpu.VMEM((2, 9, chans, chans), bf16),
                pltpu.VMEM((rows, width, chans), bf16),
                dma((3,)), dma((2, chunks)), dma((1,)),
                dma((2,)), dma((chunks,)), dma((chunks,)),
                dma((chunks,)), dma((chunks,)), dma((chunks,)), dma((chunks,)),
                dma((2, n_hi)), dma((2, n_hi)), dma((2, n_hi)), dma((2, n_hi)),
                dma((2, n_hi, 2)), dma((2, n_hi, 2)),
            ],
            compiler_params=pltpu.CompilerParams(
                collective_id=0, has_side_effects=True, vmem_limit_bytes=60 << 20
            ),
            name="context_module",
        )(features, weight_one, weight_two, offset_one.reshape(1, chans), offset_two.reshape(1, chans))

    return jax.shard_map(
        per_device,
        mesh=mesh,
        in_specs=(
            P("sample", "space", None, None),
            P(None, None, None, "sample"),
            P(),
            P(None, None, None, "sample"),
            P(),
        ),
        out_specs=P("sample", "space", None, None),
        check_vma=False,
    )
```

time: 147 us -> 45.9 us (0.31)
  the two profiles are of different devices: /device:TPU:1 before, /device:TPU:31 now
where the time goes in v1:
time: 45.9 us; the launch traced here: 45.7 us
  Pallas kernels  38.6 us (84%)
  local copies, waits for them, and re-layouts  7.03 us (15%)
    pallas_call x1, Pallas kernels, per_device(): pl.pallas_call(functools.partial(kernel, n_sample, n_space), out_shape=ja...  38.6 us
    unnamed x3, local copies, waits for them, and re-layouts  7.03 us

profile of v1, /device:TPU:31, one launch (start us, length us, event | category | flops | bytes accessed | tf_op | source)
XLA Modules:
  0.0 45.7 jit_solution(16893854549731550343)
XLA Ops:
  0.0 2.0 %copy.6.w1_ref = bf16[3,3,256,32]{3,2,1,0:T(8,128)(2,1)} copy(bf16[3,3,256,32]{2,3,1,0:T(8,128)(2,1)} %param.6) | data formatting | bytes 294912 | tf_op args[1]
  2.0 2.0 %copy.7.w2_ref = bf16[3,3,256,32]{3,2,1,0:T(8,128)(2,1)} copy(bf16[3,3,256,32]{2,3,1,0:T(8,128)(2,1)} %param.8) | data formatting | bytes 294912 | tf_op args[3]
  3.9 38.6 %context_module.1 = bf16[1,16,256,256]{3,2,1,0:T(8,128)(2,1)} custom-call(bf16[1,16,256,256]{3,2,1,0:T(8,128)(2,1)} %f_ref.1, bf16[3,3,256,32]{3,2,1,0:T(8,128)(2,1)} %copy.6.w1_ref, bf16[3,3,256,32]{3,2,1,0:T(8,128)(2,1)} %copy.7.w2_ref, f32[1,256]{1,0:T(1,128)} %bitcast.2, f32[1,256]{1,0:T(1,128)} %bitcast.3), custom_call_target="tpu_custom_call" | custom-call | tf_op jit(solution)/shard_map/context_module/pallas_call | solution.py:273
  42.6 3.1 %copy.9 = bf16[1,16,256,256]{3,2,1,0:T(8,128)(2,1)} copy(bf16[1,16,256,256]{3,2,1,0:T(8,128)(2,1)} %context_module.1) | data formatting | bytes 4194304

commit v2 on v1

--- a/solution.py
+++ b/solution.py
@@ -14,15 +14,15 @@
 
 def kernel(
     n_sample, n_space, f_ref, w1_ref, w2_ref, b1_ref, b2_ref, out_ref,
-    x, h, wloc, wt, obuf,
-    loc_sem, out_sem, bar_unused,
+    x, h, wt, obuf, loc_sem, out_sem,
     near_sem, far_s, far_r, hnear_s, hnear_r, hfar_s, hfar_r,
     z_s, z_r, y_s, y_r, c_s, c_r,
 ):
     rows, width, chans = out_ref.shape[1:]
     chunks = D // R
     n_hi = n_sample // 2
-    o_loc = wloc.shape[-1]
+    o_loc = w1_ref.shape[1]
+    weights = (w1_ref, w2_ref)
     half = chans // 2
     space = lax.axis_index("space")
     sample = lax.axis_index("sample")
@@ -36,10 +36,8 @@
     far_halo, near_halo = 3 * D * odd, 3 * D * (1 - odd)
 
     feat_in = pltpu.make_async_copy(f_ref.at[0], x.at[pl.ds(D, rows)], loc_sem.at[0])
-    w_in = [
-        pltpu.make_async_copy(w, wloc.at[l], loc_sem.at[1 + l])
-        for l, w in enumerate((w1_ref, w2_ref))
-    ]
+    own = pl.ds(pl.multiple_of(sample * o_loc, o_loc), o_loc)
+    w_in = [pltpu.make_async_copy(w, wt.at[l, :, own], loc_sem.at[1 + l]) for l, w in enumerate(weights)]
     w_in[0].start()
     w_in[1].start()
     feat_in.start()
@@ -103,9 +101,11 @@
         lane = pl.multiple_of(which * half, half)
         return wt.at[l, :, pl.ds(start, o_loc), pl.ds(lane, half)]
 
+    def shard(l):
+        return weights[l].at[:, :, pl.ds(pl.multiple_of(odd * half, half), half)]
+
     def z_copy(l, k):
-        ref = piece(l, 0, 0, odd)
-        return remote(ref, ref, z_s.at[l, k], z_r.at[l, k], {"sample": lax.rem(hi + k, n_hi) * 2 + lo})
+        return remote(shard(l), piece(l, 0, 0, odd), z_s.at[l, k], z_r.at[l, k], {"sample": lax.rem(hi + k, n_hi) * 2 + lo})
 
     def z_arrived(l, k):
         ref = piece(l, k, 0, odd)
@@ -113,7 +113,7 @@
 
     def y_copy(l, k):
         ref = piece(l, k, 0, odd)
-        return remote(ref, ref, y_s.at[l, k], y_r.at[l, k], {"sample": hi * 2 + 1 - lo})
+        return remote(ref if k else shard(l), ref, y_s.at[l, k], y_r.at[l, k], {"sample": hi * 2 + 1 - lo})
 
     def y_arrived(l, k):
         ref = piece(l, k, 1, odd)
@@ -128,11 +128,6 @@
         return remote(ref, ref, c_s.at[l, k, q], c_r.at[l, k, q], {"space": near})
 
     def scatter(l):
-        w_in[l].wait()
-        start = pl.multiple_of(sample * o_loc, o_loc)
-        for a in range(3):
-            for b in range(3):
-                wt[l, 3 * a + b, pl.ds(start, o_loc), :] = wloc[l, a, b].T
         for k in range(1, n_hi):
             z_copy(l, k).start()
         y_copy(l, 0).start()
@@ -149,6 +144,7 @@
             c_copy(l, k, 1).start()
 
     def collect(l):
+        w_in[l].wait()
         for k in range(n_hi):
             for q in range(2):
                 if (k, q) != (0, 0):
@@ -267,6 +263,10 @@
         assert features.shape[0] == 1 and rows == 2 * D
         o_loc = weight_one.shape[-1]
         n_hi, chunks = n_sample // 2, D // R
+
+        def taps(weight):
+            return jnp.swapaxes(weight, 2, 3).reshape(9, o_loc, chans)
+
         bf16, dma = jnp.bfloat16, pltpu.SemaphoreType.DMA
         anywhere = pl.BlockSpec(memory_space=pl.ANY)
         vmem = pl.BlockSpec(memory_space=pltpu.VMEM)
@@ -278,10 +278,9 @@
             scratch_shapes=[
                 pltpu.VMEM((4 * D, width, chans), bf16),
                 pltpu.VMEM((4 * D, width, chans), bf16),
-                pltpu.VMEM((2, 3, 3, chans, o_loc), bf16),
                 pltpu.VMEM((2, 9, chans, chans), bf16),
                 pltpu.VMEM((rows, width, chans), bf16),
-                dma((3,)), dma((2, chunks)), dma((1,)),
+                dma((3,)), dma((2, chunks)),
                 dma((2,)), dma((chunks,)), dma((chunks,)),
                 dma((chunks,)), dma((chunks,)), dma((chunks,)), dma((chunks,)),
                 dma((2, n_hi)), dma((2, n_hi)), dma((2, n_hi)), dma((2, n_hi)),
@@ -291,7 +290,7 @@
                 collective_id=0, has_side_effects=True, vmem_limit_bytes=60 << 20
             ),
             name="context_module",
-        )(features, weight_one, weight_two, offset_one.reshape(1, chans), offset_two.reshape(1, chans))
+        )(features, taps(weight_one), taps(weight_two), offset_one.reshape(1, chans), offset_two.reshape(1, chans))
 
     return jax.shard_map(
         per_device,

time: 45.9 us -> 41.9 us (0.913)
  the two profiles are of different devices: /device:TPU:31 before, /device:TPU:27 now
where the time goes in v2:
time: 41.9 us; the launch traced here: 41.8 us
  Pallas kernels  38.7 us (92%)
  local copies, waits for them, and re-layouts  3.1 us (7%)
    pallas_call x1, Pallas kernels, per_device(): pl.pallas_call(functools.partial(kernel, n_sample, n_space), out_shape=ja...  38.7 us
    unnamed x1, local copies, waits for them, and re-layouts  3.1 us

profile of v2, /device:TPU:27, one launch (start us, length us, event | category | flops | bytes accessed | tf_op | source)
XLA Modules:
  0.0 41.8 jit_solution(5094622199387137628)
XLA Ops:
  0.0 38.7 %context_module.1 = bf16[1,16,256,256]{3,2,1,0:T(8,128)(2,1)} custom-call(bf16[1,16,256,256]{3,2,1,0:T(8,128)(2,1)} %f_ref.1, bf16[9,32,256]{2,1,0:T(8,128)(2,1)} %bitcast.8, bf16[9,32,256]{2,1,0:T(8,128)(2,1)} %bitcast.9, f32[1,256]{1,0:T(1,128)} %bitcast.10, f32[1,256]{1,0:T(1,128)} %bitcast.11), custom_call_target="tpu_custom_call" | custom-call | tf_op jit(solution)/shard_map/context_module/pallas_call | solution.py:273
  38.7 3.1 %copy.7 = bf16[1,16,256,256]{3,2,1,0:T(8,128)(2,1)} copy(bf16[1,16,256,256]{3,2,1,0:T(8,128)(2,1)} %context_module.1) | data formatting | bytes 4194304

commit v3 on v2

--- a/solution.py
+++ b/solution.py
@@ -10,6 +10,7 @@
 MESH = pl.DeviceIdType.MESH
 D = 8
 R = 2
+B = 4
 
 
 def kernel(
@@ -85,8 +86,8 @@
 
     def hid_near(i):
         return remote(
-            h.at[pl.ds(D * near_group + R * i, R)],
-            h.at[pl.ds(3 * D * odd + R * i, R)],
+            h.at[pl.ds(D * near_group + B * i, B)],
+            h.at[pl.ds(3 * D * odd + B * i, B)],
             hnear_s.at[i], hnear_r.at[i], {"space": near},
         )
 
@@ -113,7 +114,7 @@
 
     def y_copy(l, k):
         ref = piece(l, k, 0, odd)
-        return remote(ref if k else shard(l), ref, y_s.at[l, k], y_r.at[l, k], {"sample": hi * 2 + 1 - lo})
+        return remote(shard(l) if isinstance(k, int) and k == 0 else ref, ref, y_s.at[l, k], y_r.at[l, k], {"sample": hi * 2 + 1 - lo})
 
     def y_arrived(l, k):
         ref = piece(l, k, 1, odd)
@@ -132,16 +133,14 @@
             z_copy(l, k).start()
         y_copy(l, 0).start()
 
-    def forward_z(l):
-        for k in range(1, n_hi):
-            z_arrived(l, k).wait_recv()
-            y_copy(l, k).start()
-            c_copy(l, k, 0).start()
-
-    def forward_y(l):
-        for k in range(n_hi):
-            y_arrived(l, k).wait_recv()
-            c_copy(l, k, 1).start()
+    def forward_z(l, k):
+        z_arrived(l, k).wait_recv()
+        y_copy(l, k).start()
+        c_copy(l, k, 0).start()
+
+    def forward_y(l, k):
+        y_arrived(l, k).wait_recv()
+        c_copy(l, k, 1).start()
 
     def collect(l):
         w_in[l].wait()
@@ -161,7 +160,6 @@
 
     scatter(0)
     feat_near.start()
-    scatter(1)
 
     @pl.when(jnp.logical_not(has_far))
     def _():
@@ -169,15 +167,18 @@
         x[pl.ds(far_halo, D)] = zero
         h[pl.ds(far_halo, D)] = zero
 
-    forward_z(0)
-    forward_y(0)
+    for k in range(1, n_hi):
+        forward_z(0, k)
+    scatter(1)
+    for k in range(n_hi):
+        forward_y(0, k)
     feat_in.wait()
     feat_near.wait_recv()
     collect(0)
 
-    def conv_rows(src, l, bias, group, i):
+    def conv_rows(src, l, bias, group, row, R):
         lhs = jnp.concatenate(
-            [src[pl.ds(D * (group + a - 1) + R * i, R)].reshape(R * width, chans) for a in range(3)], axis=1
+            [src[pl.ds(D * (group + a - 1) + row, R)].reshape(R * width, chans) for a in range(3)], axis=1
         )
         ys = []
         for b in range(3):
@@ -195,20 +196,30 @@
         def _():
             feat_far(i).wait_recv()
 
-        h[pl.ds(D * far_group + R * i, R)] = conv_rows(x, 0, b1_ref, far_group, i)
+        h[pl.ds(D * far_group + R * i, R)] = conv_rows(x, 0, b1_ref, far_group, R * i, R)
 
         @pl.when(has_far)
         def _():
             hid_far(i).start()
 
+        per = n_hi // chunks
+        for j in range(per):
+
+            @pl.when(i * per + j > 0)
+            def _():
+                forward_z(1, i * per + j)
+
         return carry
 
     def hidden_near(i, carry):
-        h[pl.ds(D * near_group + R * i, R)] = conv_rows(x, 0, b1_ref, near_group, i)
+        h[pl.ds(D * near_group + B * i, B)] = conv_rows(x, 0, b1_ref, near_group, B * i, B)
         hid_near(i).start()
+        per = n_hi // (D // B)
+        for j in range(per):
+            forward_y(1, i * per + j)
         return carry
 
-    def put(group, i):
+    def put(group, i, R):
         row = D * (group - 1) + R * i
         return pltpu.make_async_copy(
             obuf.at[pl.ds(row, R)], out_ref.at[0, pl.ds(row, R)], out_sem.at[group - 1, i]
@@ -216,8 +227,8 @@
 
     def context_near(i, carry):
         hid_near(i).wait_recv()
-        obuf[pl.ds(D * (near_group - 1) + R * i, R)] = conv_rows(h, 1, b2_ref, near_group, i)
-        put(near_group, i).start()
+        obuf[pl.ds(D * (near_group - 1) + B * i, B)] = conv_rows(h, 1, b2_ref, near_group, B * i, B)
+        put(near_group, i, B).start()
         return carry
 
     def context_far(i, carry):
@@ -225,22 +236,20 @@
         def _():
             hid_far(i).wait_recv()
 
-        obuf[pl.ds(D * (far_group - 1) + R * i, R)] = conv_rows(h, 1, b2_ref, far_group, i)
-        put(far_group, i).start()
+        obuf[pl.ds(D * (far_group - 1) + R * i, R)] = conv_rows(h, 1, b2_ref, far_group, R * i, R)
+        put(far_group, i, R).start()
         return carry
 
     lax.fori_loop(0, chunks, hidden_far, 0)
-    forward_z(1)
-    lax.fori_loop(0, chunks, hidden_near, 0)
-    forward_y(1)
+    lax.fori_loop(0, D // B, hidden_near, 0)
     collect(1)
-    lax.fori_loop(0, chunks, context_near, 0)
+    lax.fori_loop(0, D // B, context_near, 0)
     lax.fori_loop(0, chunks, context_far, 0)
 
     feat_near.wait_send()
     sent(0)
     sent(1)
-    for i in range(chunks):
+    for i in range(D // B):
         hid_near(i).wait_send()
 
     @pl.when(has_far)
@@ -249,9 +258,10 @@
             feat_far(i).wait_send()
             hid_far(i).wait_send()
 
+    for i in range(D // B):
+        put(near_group, i, B).wait()
     for i in range(chunks):
-        put(near_group, i).wait()
-        put(far_group, i).wait()
+        put(far_group, i, R).wait()
 
 
 def solution(mesh):

time: 41.9 us -> 38.1 us (0.909)
  the two profiles are of different devices: /device:TPU:27 before, /device:TPU:1 now
where the time goes in v3:
time: 38.1 us; the launch traced here: 37.6 us
  Pallas kernels  34.5 us (91%)
  local copies, waits for them, and re-layouts  3.1 us (8%)
    pallas_call x1, Pallas kernels, per_device(): pl.pallas_call(functools.partial(kernel, n_sample, n_space), out_shape=ja...  34.5 us
    unnamed x1, local copies, waits for them, and re-layouts  3.1 us

profile of v3, /device:TPU:1, one launch (start us, length us, event | category | flops | bytes accessed | tf_op | source)
XLA Modules:
  0.0 37.6 jit_solution(11877606057639208533)
XLA Ops:
  0.0 34.5 %context_module.1 = bf16[1,16,256,256]{3,2,1,0:T(8,128)(2,1)} custom-call(bf16[1,16,256,256]{3,2,1,0:T(8,128)(2,1)} %f_ref.1, bf16[9,32,256]{2,1,0:T(8,128)(2,1)} %bitcast.8, bf16[9,32,256]{2,1,0:T(8,128)(2,1)} %bitcast.9, f32[1,256]{1,0:T(1,128)} %bitcast.10, f32[1,256]{1,0:T(1,128)} %bitcast.11), custom_call_target="tpu_custom_call" | custom-call | tf_op jit(solution)/shard_map/context_module/pallas_call | solution.py:283
  34.6 3.1 %copy.7 = bf16[1,16,256,256]{3,2,1,0:T(8,128)(2,1)} copy(bf16[1,16,256,256]{3,2,1,0:T(8,128)(2,1)} %context_module.1) | data formatting | bytes 4194304

commit v4 on v3

--- a/solution.py
+++ b/solution.py
@@ -14,12 +14,12 @@
 
 
 def kernel(
-    n_sample, n_space, f_ref, w1_ref, w2_ref, b1_ref, b2_ref, out_ref,
-    x, h, wt, obuf, loc_sem, out_sem,
+    n_sample, n_space, f_ref, w1_ref, w2_ref, b1_ref, b2_ref, obuf,
+    x, h, wt, loc_sem,
     near_sem, far_s, far_r, hnear_s, hnear_r, hfar_s, hfar_r,
     z_s, z_r, y_s, y_r, c_s, c_r,
 ):
-    rows, width, chans = out_ref.shape[1:]
+    rows, width, chans = obuf.shape
     chunks = D // R
     n_hi = n_sample // 2
     o_loc = w1_ref.shape[1]
@@ -228,7 +228,6 @@
     def context_near(i, carry):
         hid_near(i).wait_recv()
         obuf[pl.ds(D * (near_group - 1) + B * i, B)] = conv_rows(h, 1, b2_ref, near_group, B * i, B)
-        put(near_group, i, B).start()
         return carry
 
     def context_far(i, carry):
@@ -237,7 +236,6 @@
             hid_far(i).wait_recv()
 
         obuf[pl.ds(D * (far_group - 1) + R * i, R)] = conv_rows(h, 1, b2_ref, far_group, R * i, R)
-        put(far_group, i, R).start()
         return carry
 
     lax.fori_loop(0, chunks, hidden_far, 0)
@@ -258,11 +256,6 @@
             feat_far(i).wait_send()
             hid_far(i).wait_send()
 
-    for i in range(D // B):
-        put(near_group, i, B).wait()
-    for i in range(chunks):
-        put(far_group, i, R).wait()
-
 
 def solution(mesh):
     n_sample, n_space = mesh.shape["sample"], mesh.shape["space"]
@@ -280,17 +273,16 @@
         bf16, dma = jnp.bfloat16, pltpu.SemaphoreType.DMA
         anywhere = pl.BlockSpec(memory_space=pl.ANY)
         vmem = pl.BlockSpec(memory_space=pltpu.VMEM)
-        return pl.pallas_call(
+        result = pl.pallas_call(
             functools.partial(kernel, n_sample, n_space),
-            out_shape=jax.ShapeDtypeStruct(features.shape, bf16),
+            out_shape=pltpu.VMEM(features.shape[1:], bf16),
             in_specs=[anywhere, anywhere, anywhere, vmem, vmem],
-            out_specs=anywhere,
+            out_specs=vmem,
             scratch_shapes=[
                 pltpu.VMEM((4 * D, width, chans), bf16),
                 pltpu.VMEM((4 * D, width, chans), bf16),
                 pltpu.VMEM((2, 9, chans, chans), bf16),
-                pltpu.VMEM((rows, width, chans), bf16),
-                dma((3,)), dma((2, chunks)),
+                dma((3,)),
                 dma((2,)), dma((chunks,)), dma((chunks,)),
                 dma((chunks,)), dma((chunks,)), dma((chunks,)), dma((chunks,)),
                 dma((2, n_hi)), dma((2, n_hi)), dma((2, n_hi)), dma((2, n_hi)),
@@ -301,6 +293,20 @@
             ),
             name="context_module",
         )(features, taps(weight_one), taps(weight_two), offset_one.reshape(1, chans), offset_two.reshape(1, chans))
+
+        def store(r_ref, o_ref, sem):
+            copy = pltpu.make_async_copy(r_ref, o_ref.at[0], sem)
+            copy.start()
+            copy.wait()
+
+        return pl.pallas_call(
+            store,
+            out_shape=jax.ShapeDtypeStruct(features.shape, bf16),
+            in_specs=[vmem],
+            out_specs=anywhere,
+            scratch_shapes=[dma],
+            name="store_context",
+        )(pltpu.with_memory_space_constraint(result, pltpu.VMEM))
 
     return jax.shard_map(
         per_device,

time: 38.1 us -> 35.6 us (0.934)
  local copies, waits for them, and re-layouts: 3.1 us -> 0 us
  Pallas kernels: 34.5 us -> 35.2 us
    unnamed x1 -> x0, local copies, waits for them, and re-layouts: 3.1 us -> none
    pallas_call x1 -> x2, Pallas kernels: 34.5 us -> 35.2 us  [the longest x1 33.8 us: per_device(): pl.pallas_call(functools.partial(kernel, n_sample, n_space), out_shape=pl...]
where the time goes in v4:
time: 35.6 us; the launch traced here: 35.2 us
  Pallas kernels  35.2 us (99%)
    pallas_call x1, Pallas kernels, per_device(): pl.pallas_call(functools.partial(kernel, n_sample, n_space), out_shape=pl...  33.8 us
    pallas_call x1, Pallas kernels, per_device(): pl.pallas_call(store, out_shape=jax.ShapeDtypeStruct(features.shape, bf16...  1.33 us

profile of v4, /device:TPU:1, one launch (start us, length us, event | category | flops | bytes accessed | tf_op | source)
XLA Modules:
  0.0 35.2 jit_solution(3166867157690577014)
XLA Ops:
  0.0 33.8 %context_module.1.r_ref = bf16[16,256,256]{2,1,0:T(8,128)(2,1)S(1)} custom-call(bf16[1,16,256,256]{3,2,1,0:T(8,128)(2,1)} %f_ref.1, bf16[9,32,256]{2,1,0:T(8,128)(2,1)} %bitcast.8, bf16[9,32,256]{2,1,0:T(8,128)(2,1)} %bitcast.9, f32[1,256]{1,0:T(1,128)} %bitcast.10, f32[1,256]{1,0:T(1,128)} %bitcast.11), custom_call_target="tpu_custom_call" | custom-call | tf_op jit(solution)/shard_map/context_module/pallas_call | solution.py:276
  33.8 1.3 %store_context.1 = bf16[1,16,256,256]{3,2,1,0:T(8,128)(2,1)} custom-call(bf16[16,256,256]{2,1,0:T(8,128)(2,1)S(1)} %context_module.1.r_ref), custom_call_target="tpu_custom_call" | custom-call | tf_op jit(solution)/shard_map/store_context/pallas_call | solution.py:302

commit v5 on v4

--- a/solution.py
+++ b/solution.py
@@ -131,7 +131,6 @@
     def scatter(l):
         for k in range(1, n_hi):
             z_copy(l, k).start()
-        y_copy(l, 0).start()
 
     def forward_z(l, k):
         z_arrived(l, k).wait_recv()
@@ -159,6 +158,7 @@
                     c_copy(l, k, q).wait_send()
 
     scatter(0)
+    y_copy(0, 0).start()
     feat_near.start()
 
     @pl.when(jnp.logical_not(has_far))
@@ -169,7 +169,9 @@
 
     for k in range(1, n_hi):
         forward_z(0, k)
-    scatter(1)
+        if k == n_hi // 2:
+            scatter(1)
+    y_copy(1, 0).start()
     for k in range(n_hi):
         forward_y(0, k)
     feat_in.wait()
@@ -230,19 +232,24 @@
         obuf[pl.ds(D * (near_group - 1) + B * i, B)] = conv_rows(h, 1, b2_ref, near_group, B * i, B)
         return carry
 
-    def context_far(i, carry):
+    def context_far(i, size):
         @pl.when(has_far)
         def _():
-            hid_far(i).wait_recv()
-
-        obuf[pl.ds(D * (far_group - 1) + R * i, R)] = conv_rows(h, 1, b2_ref, far_group, R * i, R)
+            for j in range(size // R):
+                hid_far(i + j).wait_recv()
+
+        obuf[pl.ds(D * (far_group - 1) + R * i, size)] = conv_rows(h, 1, b2_ref, far_group, R * i, size)
+
+    def context_far_end(i, carry):
+        context_far(i, R)
         return carry
 
     lax.fori_loop(0, chunks, hidden_far, 0)
     lax.fori_loop(0, D // B, hidden_near, 0)
     collect(1)
     lax.fori_loop(0, D // B, context_near, 0)
-    lax.fori_loop(0, chunks, context_far, 0)
+    context_far(0, B)
+    lax.fori_loop(B // R, chunks, context_far_end, 0)
 
     feat_near.wait_send()
     sent(0)

time: 35.6 us -> 35.4 us (level)
  no operation moved by 1% of the time
where the time goes in v5:
time: 35.4 us; the launch traced here: 35.2 us
  Pallas kernels  35.2 us (99%)
    pallas_call x1, Pallas kernels, per_device(): pl.pallas_call(functools.partial(kernel, n_sample, n_space), out_shape=pl...  33.8 us
    pallas_call x1, Pallas kernels, per_device(): pl.pallas_call(store, out_shape=jax.ShapeDtypeStruct(features.shape, bf16...  1.33 us

profile of v5, /device:TPU:1, one launch (start us, length us, event | category | flops | bytes accessed | tf_op | source)
XLA Modules:
  0.0 35.2 jit_solution(6911308197055547054)
XLA Ops:
  0.0 33.8 %context_module.1.r_ref = bf16[16,256,256]{2,1,0:T(8,128)(2,1)S(1)} custom-call(bf16[1,16,256,256]{3,2,1,0:T(8,128)(2,1)} %f_ref.1, bf16[9,32,256]{2,1,0:T(8,128)(2,1)} %bitcast.8, bf16[9,32,256]{2,1,0:T(8,128)(2,1)} %bitcast.9, f32[1,256]{1,0:T(1,128)} %bitcast.10, f32[1,256]{1,0:T(1,128)} %bitcast.11), custom_call_target="tpu_custom_call" | custom-call | tf_op jit(solution)/shard_map/context_module/pallas_call | solution.py:283
  33.8 1.3 %store_context.1 = bf16[1,16,256,256]{3,2,1,0:T(8,128)(2,1)} custom-call(bf16[16,256,256]{2,1,0:T(8,128)(2,1)S(1)} %context_module.1.r_ref), custom_call_target="tpu_custom_call" | custom-call | tf_op jit(solution)/shard_map/store_context/pallas_call | solution.py:309
